TPU v7x, 32 devices: a whole 2x2x4 slice. The times are simulated.
32 devices in a mesh: dp: 8 (over z, y), tp: 4 (over x, core).
Axes of the slice: x: 2, y: 2, z: 4, core: 2. Of those that a mesh axis runs over, the one named last changes fastest.
Arguments:
- tokens: bfloat16 [8, 2048, 768], P('dp', 'tp'), may hold values from -6 to 6
- cotangent: bfloat16 [8, 2048, 768], P('dp', 'tp'), may hold values from -6 to 6
- tags: int32 [8], P('dp'), may hold values from 0 to 7
- tag_weight: float32 [8], replicated, may hold values from 0.25 to 4
- query_weight: bfloat16 [768, 768], P(None, 'tp'), may hold values from -0.21875 to 0.21875
- key_value_weight: bfloat16 [768, 128], replicated, may hold values from -0.21875 to 0.21875
- output_weight: bfloat16 [768, 768], P('tp'), may hold values from -1.25 to 1.25
- up_weight: bfloat16 [768, 3072], P(None, 'tp'), may hold values from -0.21875 to 0.21875
- down_weight: bfloat16 [3072, 768], P('tp'), may hold values from -0.109375 to 0.109375
- norm_gain_one: float32 [768], replicated, may hold values from 0.25 to 1.75
- norm_bias_one: float32 [768], replicated, may hold values from -1.5 to 1.5
- norm_gain_two: float32 [768], replicated, may hold values from 0.25 to 1.75
- norm_bias_two: float32 [768], replicated, may hold values from -1.5 to 1.5
Outputs:
- block_out: bfloat16 [8, 2048, 768], P('dp', 'tp')
- grad_tokens: bfloat16 [8, 2048, 768], P('dp', 'tp')
- grad_query: float32 [768, 768], P(None, 'tp')
- grad_keyval: float32 [768, 128], replicated
- grad_output: float32 [768, 768], P('tp')
- grad_upward: float32 [768, 3072], P(None, 'tp')
- grad_downward: float32 [3072, 768], P('tp')
- grad_gain_one: float32 [768], replicated
- grad_bias_one: float32 [768], replicated
- grad_gain_two: float32 [768], replicated
- grad_bias_two: float32 [768], replicated
All inputs are finite; a program needn't handle non-finite values.
Results may differ from a plain program's by a relative error of at most 0.013.
Values may be sent and summed in bfloat16 or wider, within the bound.
A program may use at most 128 MiB of HBM per device.

v0:
```python
import jax
import jax.numpy as jnp
from jax import lax
from jax.sharding import PartitionSpec as P

HD = 64
ROT = 16


def layer_norm(values, gain_vec, shift_vec):
    row_mean = jnp.mean(values, axis=-1, keepdims=True)
    centred = values - row_mean
    variance = jnp.mean(centred * centred, axis=-1, keepdims=True)
    inverse = lax.rsqrt(variance + 1e-05)
    normal = centred * inverse
    return (normal * gain_vec + shift_vec, normal, inverse)


def norm_back(scaled, normal, inverse):
    term_one = jnp.mean(scaled, axis=-1, keepdims=True)
    term_two = jnp.mean(scaled * normal, axis=-1, keepdims=True)
    return inverse * (scaled - term_one - normal * term_two)


def rot_angles(positions):
    frequencies = 10000.0 ** (-jnp.arange(0, ROT, 2, dtype=jnp.float32) / ROT)
    return positions.astype(jnp.float32)[:, None] * frequencies[None, :]


def rotate(values, angles, direction):
    half_rot = ROT // 2
    cosine = jnp.cos(angles)[:, None, :]
    sine_part = direction * jnp.sin(angles)[:, None, :]
    front_half = values[..., :half_rot]
    back_half = values[..., half_rot:ROT]
    return jnp.concatenate(
        [
            front_half * cosine - back_half * sine_part,
            back_half * cosine + front_half * sine_part,
            values[..., ROT:],
        ],
        axis=-1,
    )


def outer_sum(left, right):
    return lax.dot_general(
        left, right, (((0, 1), (0, 1)), ((), ())), preferred_element_type=jnp.float32
    )


def against(left, weight):
    return lax.dot_general(
        left, weight, (((2,), (1,)), ((), ())), preferred_element_type=jnp.float32
    )


def shards(
    tokens,
    cotangent,
    tags,
    tag_weight,
    query_weight,
    key_value_weight,
    output_weight,
    up_weight,
    down_weight,
    norm_gain_one,
    norm_bias_one,
    norm_gain_two,
    norm_bias_two,
):
    seq_dev, own_len, model_width = tokens.shape
    full_len = own_len * lax.axis_size("tp")
    heads_dev = query_weight.shape[1] // HD
    score_scale = HD ** (-0.5)
    block_rows = min(512, full_len)
    blocks = full_len // block_rows
    own_rows = tokens.astype(jnp.float32)
    full_angles = rot_angles(jnp.arange(full_len))
    tag_ids = jnp.arange(tag_weight.shape[0], dtype=jnp.int32)
    row_weight = jnp.sum(
        jnp.where(tags[:, None] == tag_ids[None, :], tag_weight[None, :], 0.0), axis=1
    )
    upstream = cotangent.astype(jnp.float32) * row_weight[:, None, None]
    all_rows = lax.all_gather(tokens, "tp", axis=1, tiled=True).astype(jnp.float32)
    grad_rows = lax.all_gather(upstream.astype(jnp.bfloat16), "tp", axis=1, tiled=True)
    normed_one, normal_all, _ = layer_norm(all_rows, norm_gain_one, norm_bias_one)
    rows_one = normed_one.astype(jnp.bfloat16)
    rows_two = (normal_all * norm_gain_two + norm_bias_two).astype(jnp.bfloat16)
    key_value_rows = jnp.dot(rows_one, key_value_weight, preferred_element_type=jnp.float32)
    key_part = rotate(key_value_rows[:, :, None, :HD], full_angles, 1.0)[:, :, 0, :]
    key_value_rows = jnp.concatenate([key_part, key_value_rows[:, :, HD:]], axis=-1).astype(
        jnp.bfloat16
    )
    key_rows = key_value_rows[:, :, :HD]
    value_rows = key_value_rows[:, :, HD:]
    query_matrix = jnp.dot(rows_one, query_weight, preferred_element_type=jnp.float32).reshape(
        seq_dev, full_len, heads_dev, HD
    )
    query_matrix = rotate(query_matrix, full_angles, 1.0).astype(jnp.bfloat16)

    def block_scores(query_block, block_start):
        block_end = block_start + block_rows
        scores = (
            jnp.einsum(
                "sqhd,skd->sqhk",
                query_block,
                key_rows[:, :block_end],
                preferred_element_type=jnp.float32,
            )
            * score_scale
        )
        allowed = jnp.arange(block_end)[None, :] <= (block_start + jnp.arange(block_rows))[:, None]
        return jnp.where(allowed[None, :, None, :], scores, -1e30)

    context_list = []
    lse_list = []
    for block_index in range(blocks):
        block_start = block_index * block_rows
        block_end = block_start + block_rows
        scores = block_scores(query_matrix[:, block_start:block_end], block_start)
        row_top = jnp.max(scores, axis=-1, keepdims=True)
        weights = jnp.exp(scores - row_top)
        row_total = jnp.sum(weights, axis=-1, keepdims=True)
        weights_low = (weights / row_total).astype(jnp.bfloat16)
        context_list.append(
            jnp.einsum(
                "sqhk,skd->sqhd",
                weights_low,
                value_rows[:, :block_end],
                preferred_element_type=jnp.float32,
            )
        )
        lse_list.append(row_top + jnp.log(row_total))
    context_full = jnp.concatenate(context_list, axis=1)
    low_context = context_full.reshape(seq_dev, full_len, heads_dev * HD).astype(jnp.bfloat16)
    attention_branch = jnp.dot(low_context, output_weight, preferred_element_type=jnp.float32)
    hidden_rows = jnp.dot(rows_two, up_weight, preferred_element_type=jnp.float32)
    middle_rows = jax.nn.gelu(hidden_rows, approximate=False).astype(jnp.bfloat16)
    feedforward_branch = jnp.dot(middle_rows, down_weight, preferred_element_type=jnp.float32)
    branch = lax.psum_scatter(
        (attention_branch + feedforward_branch).astype(jnp.bfloat16),
        "tp",
        scatter_dimension=1,
        tiled=True,
    ).astype(jnp.float32)
    block_out = (own_rows + branch).astype(jnp.bfloat16)
    grad_output = outer_sum(low_context, grad_rows)
    grad_downward = outer_sum(middle_rows, grad_rows)
    grad_context = (
        against(grad_rows, output_weight)
        .astype(jnp.bfloat16)
        .reshape(seq_dev, full_len, heads_dev, HD)
    )
    grad_middle = against(grad_rows, down_weight)
    normal_cdf = 0.5 * (1.0 + lax.erf(hidden_rows * 0.7071067811865476))
    density = jnp.exp(-0.5 * hidden_rows * hidden_rows) * 0.3989422804014327
    grad_hidden = (grad_middle * (normal_cdf + hidden_rows * density)).astype(jnp.bfloat16)
    grad_upward = outer_sum(rows_two, grad_hidden)
    norm_part_two = against(grad_hidden, up_weight)
    grad_kv_full = jnp.zeros((seq_dev, full_len, 2 * HD), jnp.float32)
    query_grad_list = []
    for block_index in range(blocks):
        block_start = block_index * block_rows
        block_end = block_start + block_rows
        query_block = query_matrix[:, block_start:block_end]
        grad_block = grad_context[:, block_start:block_end]
        scores = block_scores(query_block, block_start)
        weights = jnp.exp(scores - lse_list[block_index])
        grad_weights = jnp.einsum(
            "sqhd,skd->sqhk",
            grad_block,
            value_rows[:, :block_end],
            preferred_element_type=jnp.float32,
        )
        row_delta = jnp.sum(
            grad_block.astype(jnp.float32) * context_list[block_index], axis=-1, keepdims=True
        )
        grad_scores = (weights * (grad_weights - row_delta)).astype(jnp.bfloat16)
        query_grad_list.append(
            jnp.einsum(
                "sqhk,skd->sqhd",
                grad_scores,
                key_rows[:, :block_end],
                preferred_element_type=jnp.float32,
            )
            * score_scale
        )
        grad_keys = (
            jnp.einsum(
                "sqhk,sqhd->skd", grad_scores, query_block, preferred_element_type=jnp.float32
            )
            * score_scale
        )
        grad_values = jnp.einsum(
            "sqhk,sqhd->skd",
            weights.astype(jnp.bfloat16),
            grad_block,
            preferred_element_type=jnp.float32,
        )
        grad_kv_full = grad_kv_full.at[:, :block_end].add(
            jnp.concatenate([grad_keys, grad_values], axis=-1)
        )
    grad_queries = jnp.concatenate(query_grad_list, axis=1)
    grad_queries = (
        rotate(grad_queries, full_angles, -1.0)
        .reshape(seq_dev, full_len, heads_dev * HD)
        .astype(jnp.bfloat16)
    )
    grad_query = outer_sum(rows_one, grad_queries)
    norm_part_one = against(grad_queries, query_weight)
    key_back = rotate(grad_kv_full[:, :, None, :HD], full_angles, -1.0)[:, :, 0, :]
    keyval_part = jnp.concatenate([key_back, grad_kv_full[:, :, HD:]], axis=-1)
    low_keyval = keyval_part.astype(jnp.bfloat16)
    grad_keyval = outer_sum(rows_one, low_keyval)
    part_one = norm_part_one + against(low_keyval, key_value_weight)
    small = jnp.stack(
        [
            jnp.sum(part_one * normal_all, axis=(0, 1)),
            jnp.sum(part_one, axis=(0, 1)),
            jnp.sum(norm_part_two * normal_all, axis=(0, 1)),
            jnp.sum(norm_part_two, axis=(0, 1)),
        ]
    )
    scaled = lax.psum_scatter(
        (part_one * norm_gain_one + norm_part_two * norm_gain_two).astype(jnp.bfloat16),
        "tp",
        scatter_dimension=1,
        tiled=True,
    ).astype(jnp.float32)
    _, normal_own, inverse_own = layer_norm(own_rows, norm_gain_one, norm_bias_one)
    grad_tokens = upstream + norm_back(scaled, normal_own, inverse_own)
    grad_query, grad_output, grad_upward, grad_downward = [
        v.astype(jnp.float32)
        for v in lax.psum(
            tuple(
                (
                    v.astype(jnp.bfloat16)
                    for v in (grad_query, grad_output, grad_upward, grad_downward)
                )
            ),
            "dp",
        )
    ]
    tail = lax.psum(
        jnp.concatenate([grad_keyval.reshape(-1), small.reshape(-1)]).reshape(-1, 128), ("dp", "tp")
    ).reshape(-1)
    grad_keyval, small = (
        tail[: grad_keyval.size].reshape(grad_keyval.shape),
        tail[grad_keyval.size :].reshape(small.shape),
    )
    grad_gain_one, grad_bias_one, grad_gain_two, grad_bias_two = small
    return (
        block_out,
        grad_tokens.astype(jnp.bfloat16),
        grad_query,
        grad_keyval,
        grad_output,
        grad_upward,
        grad_downward,
        grad_gain_one,
        grad_bias_one,
        grad_gain_two,
        grad_bias_two,
    )


def solution(mesh):
    in_specs = (
        P("dp", "tp", None),
        P("dp", "tp", None),
        P("dp"),
        P(),
        P(None, "tp"),
        P(),
        P("tp", None),
        P(None, "tp"),
        P("tp", None),
        P(),
        P(),
        P(),
        P(),
    )
    out_specs = (
        P("dp", "tp", None),
        P("dp", "tp", None),
        P(None, "tp"),
        P(),
        P("tp", None),
        P(None, "tp"),
        P("tp", None),
        P(),
        P(),
        P(),
        P(),
    )
    return jax.shard_map(shards, mesh=mesh, in_specs=in_specs, out_specs=out_specs, check_vma=False)
```

profile of v0, /device:TPU:0, one launch (start us, length us, event | category | flops | bytes accessed | tf_op | source)
XLA Modules:
  0.0 513.2 jit_solution(20159249226310110)
XLA Ops:
  9.9 2.8 fusion.102
  17.0 23.9 %all-gather.3.cloned.1.call-done = bf16[1,2048,768]{2,1,0:T(8,128)(2,1)} async-done(((bf16[1,512,768]{2,1,0:T(8,128)(2,1)}), bf16[1,2048,768]{2,1,0:T(8,128)(2,1)}) %all-gather.3.cloned.1.call-update) | async-done | bytes 3145744 | tf_op jit(solution)/shard_map/all_gather | solution.py:86
  40.9 2.5 convert_reduce_fusion
  43.4 2.9 fusion.17
  61.7 6.2 %fusion.10 = (f32[512,3]{0,1:T(4,128)S(1)}, f32[512,3,2048]{2,0,1:T(8,128)}) fusion(pred[512,2048]{1,0:T(8,128)(4,1)S(1)} %iota_compare_fusion, bf16[1,2048,1,48]{1,3,2,0:T(8,128)(2,1)S(1)} %slice.387, bf16[1,2048,1,8]{1,3,2,0:T(8,128)(2,1)S(1)} %get-tuple-element.92, bf16[1,2048,1,8]{1,3,2,0:T(8,128)(2,1)S(1)} %get-tuple-element.91, ...), kind=kOutput, calls=%fused_computation.25 | convolution fusion | flops 412875264 | bytes 14096384 | tf_op jit(solution)/shard_map/sqhd,skd->sqhk/dot_general | solution.py:106
  70.5 6.9 %fusion = f32[512,3]{0,1:T(4,128)S(1)} fusion(f32[512,3,2048]{2,0,1:T(8,128)} %get-tuple-element.109, f32[512,3]{0,1:T(4,128)S(1)} %get-tuple-element.108, pred[512,2048]{1,0:T(8,128)(4,1)S(1)} %iota_compare_fusion), kind=kLoop, calls=%fused_computation.6 | loop fusion | flops 12581376 | bytes 13643776 | tf_op jit(solution)/shard_map/reduce_sum | solution.py:125
  78.6 3.1 fusion.194
  82.2 2.9 fusion.193
  86.2 4.8 fusion.192
  91.0 3.1 fusion.71
  94.2 7.3 %fusion.80 = f32[1,2048,64]{1,2,0:T(8,128)} fusion(f32[512,3,2048]{2,0,1:T(8,128)} %get-tuple-element.109, f32[512,3]{0,1:T(4,128)S(1)} %copy-done.50, pred[512,2048]{1,0:T(8,128)(4,1)S(1)} %iota_compare_fusion, bf16[1,2048,3,64]{1,3,2,0:T(8,128)(2,1)S(1)} %bitcast.290), kind=kOutput, calls=%fused_computation.113 | convolution fusion | flops 415236096 | bytes 14360576 | tf_op jit(solution)/shard_map/sqhk,sqhd->skd/dot_general | solution.py:196
  101.6 2.0 fusion.132
  104.4 4.6 multiply_convert_fusion
  109.1 2.0 fusion.115
  117.3 2.4 multiply_convert_fusion.2
  123.2 2.5 multiply_convert_fusion.1
  130.1 17.6 %fusion.20 = (bf16[2048,768]{1,0:T(8,128)(2,1)}, f32[2048,768]{1,0:T(8,128)S(1)}) fusion(bf16[768,768]{1,0:T(8,128)(2,1)S(1)} %copy-done, bf16[1,2048,768]{2,1,0:T(8,128)(2,1)S(1)} %copy-done.3, f32[768]{0:T(1024)S(1)} %copy-done.59, f32[768]{0:T(1024)S(1)} %copy-done.55, f32[2048]{0:T(1024)S(1)} %copy-done.40, f32[2048]{0:T(1024)S(1)} %broadcast_multiply_fusion.1), kind=kOutput, calls=%fused_computation.35 | convolution fusion | flops 2527592448 | bytes 13785088 | tf_op jit(solution)/shard_map/dot_general | solution.py:139
  147.7 5.2 %fusion.26 = bf16[2048,768]{1,0:T(8,128)(2,1)S(1)} fusion(f32[2048,768]{1,0:T(8,128)S(1)} %get-tuple-element.112, bf16[768,768]{1,0:T(8,128)(2,1)S(1)} %copy-done.58, bf16[1,2048,768]{2,1,0:T(8,128)(2,1)S(1)} %copy-done.56), kind=kOutput, calls=%fused_computation.41 | convolution fusion | flops 2431647744 | bytes 13762560 | tf_op jit(solution)/shard_map/dot_general | solution.py:53
  152.9 2.7 fusion.197
  158.8 3.0 fusion.15
  161.8 2.9 fusion.188
  165.8 7.1 %convolution_convert_fusion = bf16[768,768]{1,0:T(8,128)(2,1)} fusion(bf16[2048,768]{1,0:T(8,128)(2,1)} %copy-done.61, bf16[1,2048,768]{2,1,0:T(8,128)(2,1)} %all-gather.3.cloned.1.call-done, f32[768]{0:T(1024)S(1)} %copy-done.59, f32[768]{0:T(1024)S(1)} %copy-done.55, f32[2048]{0:T(1024)S(1)} %copy-done.40, f32[2048]{0:T(1024)S(1)} %broadcast_multiply_fusion.1), kind=kOutput, calls=%fused_computation.143 | convolution fusion | flops 2425946112 | bytes 7493632 | tf_op jit(solution)/shard_map/dot_general | solution.py:47
  173.0 3.7 fusion.104
  180.6 4.9 fusion.195
  185.5 2.7 fusion.65
  188.8 102.7 %all-reduce.5.cloned.1.call-done = f32[792,128]{1,0:T(8,128)} async-done(((f32[792,128]{1,0:T(8,128)}), f32[792,128]{1,0:T(8,128)}) %all-reduce.5.cloned.1.call-update) | async-done | bytes 405520 | tf_op jit(solution)/shard_map/psum | solution.py:246
  294.7 127.7 %all-reduce.7.cloned.1.call-done = (bf16[768,192]{0,1:T(8,128)(2,1)}, bf16[192,768]{1,0:T(8,128)(2,1)}, bf16[768,768]{1,0:T(8,128)(2,1)}, bf16[768,768]{1,0:T(8,128)(2,1)}) async-done(((bf16[768,192]{0,1:T(8,128)(2,1)}, bf16[192,768]{1,0:T(8,128)(2,1)}, bf16[768,768]{1,0:T(8,128)(2,1)}, bf16[768,768]{1,0:T(8,128)(2,1)}), (bf16[768,192]{0,1:T(8,128)(2,1)}, bf16[192,768]{1,0:T(8,128)(2,1)}, ...) | async-done | bytes 2949136 | tf_op jit(solution)/shard_map/psum | solution.py:236
  426.1 2.8 convert_element_type.267
  428.9 2.9 convert_element_type.269
  431.8 29.9 %reduce-scatter.5.cloned.1.call-done = bf16[1,512,768]{2,1,0:T(8,128)(2,1)} async-done(((bf16[1,2048,768]{2,1,0:T(8,128)(2,1)}), bf16[1,512,768]{2,1,0:T(8,128)(2,1)}) %reduce-scatter.5.cloned.1.call-update) | async-done | bytes 786448 | tf_op jit(solution)/shard_map/reduce_scatter | solution.py:226
  463.6 38.7 %reduce-scatter.3.cloned.1.call-done = bf16[1,512,768]{2,1,0:T(8,128)(2,1)} async-done(((bf16[1,2048,768]{2,1,0:T(8,128)(2,1)}), bf16[1,512,768]{2,1,0:T(8,128)(2,1)}) %reduce-scatter.3.cloned.1.call-update) | async-done | bytes 786448 | tf_op jit(solution)/shard_map/reduce_scatter | solution.py:142
  502.2 3.8 fusion.93
  (253 shorter events, 58.7 us)
Async XLA Ops:
  7.2 122.1 %copy-start = (bf16[768,768]{1,0:T(8,128)(2,1)S(1)}, bf16[768,768]{1,0:T(8,128)(2,1)}, u32[]{:S(2)}) copy-start(bf16[768,768]{1,0:T(8,128)(2,1)} %param.30) | copy-start | bytes 3538948
  7.2 39.8 %copy-start.46 = (f32[768]{0:T(1024)S(1)}, f32[768]{0:T(1024)}, u32[]{:S(2)}) copy-start(f32[768]{0:T(1024)} %param.32) | copy-start | bytes 9220
  7.2 39.8 %copy-start.54 = (f32[768]{0:T(1024)S(1)}, f32[768]{0:T(1024)}, u32[]{:S(2)}) copy-start(f32[768]{0:T(1024)} %param.33) | copy-start | bytes 9220
  7.2 33.7 %all-gather.3.cloned.1.call-start = ((), (), s32[]{:S(2)}) async-start(), calls=%async_computation.2 | async-start | bytes 3932160 | tf_op jit(solution)/shard_map/all_gather | solution.py:86
  7.9 83.1 %all-gather.5.cloned.1.call-start = ((), (), s32[]{:S(2)}) async-start(), calls=%async_computation.4 | async-start | bytes 3932160 | tf_op jit(solution)/shard_map/all_gather | solution.py:87
  12.7 278.8 %all-reduce.5.cloned.1.call-start = ((), (), s32[]{:S(2)}) async-start(), calls=%async_computation.6 | async-start | bytes 811008 | tf_op jit(solution)/shard_map/psum | solution.py:246
  12.8 28.1 %copy-start.51 = (f32[8]{0:T(128)}, f32[8]{0:T(128)S(1)}, u32[]{:S(2)}) copy-start(f32[8]{0:T(128)S(1)} %multiply_power_fusion) | copy-start | bytes 100
  17.0 35.2 %copy-start.18 = (f32[2048,8]{0,1:T(8,128)}, f32[2048,8]{0,1:T(8,128)S(1)}, u32[]{:S(2)}) copy-start(f32[2048,8]{0,1:T(8,128)S(1)} %get-tuple-element.99) | copy-start | bytes 196612
  17.0 31.5 %copy-start.20 = (bf16[768,128]{1,0:T(8,128)(2,1)S(1)}, bf16[768,128]{1,0:T(8,128)(2,1)}, u32[]{:S(2)}) copy-start(bf16[768,128]{1,0:T(8,128)(2,1)} %param.28) | copy-start | bytes 589828
  50.9 10.8 %copy-start.25 = (bf16[1,2048,1,8]{1,3,2,0:T(8,128)(2,1)}, bf16[1,2048,1,8]{1,3,2,0:T(8,128)(2,1)S(1)}, u32[]{:S(2)}) copy-start(bf16[1,2048,1,8]{1,3,2,0:T(8,128)(2,1)S(1)} %get-tuple-element.91) | copy-start | bytes 98308
  50.9 10.8 %copy-start.27 = (bf16[1,2048,1,8]{1,3,2,0:T(8,128)(2,1)}, bf16[1,2048,1,8]{1,3,2,0:T(8,128)(2,1)S(1)}, u32[]{:S(2)}) copy-start(bf16[1,2048,1,8]{1,3,2,0:T(8,128)(2,1)S(1)} %get-tuple-element.92) | copy-start | bytes 98308
  50.9 10.8 %copy-start.12 = (bf16[1,2048,1,48]{1,3,2,0:T(8,128)(2,1)}, bf16[1,2048,1,48]{1,3,2,0:T(8,128)(2,1)S(1)}, u32[]{:S(2)}) copy-start(bf16[1,2048,1,48]{1,3,2,0:T(8,128)(2,1)S(1)} %slice.387) | copy-start | bytes 589828
  52.4 7.3 %copy-start.14 = (bf16[1,2048,64]{1,2,0:T(8,128)(2,1)}, bf16[1,2048,64]{1,2,0:T(8,128)(2,1)S(1)}, u32[]{:S(2)}) copy-start(bf16[1,2048,64]{1,2,0:T(8,128)(2,1)S(1)} %fusion.184) | copy-start | bytes 786436
  57.1 21.4 %copy-start.10 = (f32[512,3,1024]{2,0,1:T(8,128)}, f32[512,3,1024]{2,0,1:T(8,128)S(1)}, u32[]{:S(2)}) copy-start(f32[512,3,1024]{2,0,1:T(8,128)S(1)} %get-tuple-element.105) | copy-start | bytes 18874372
  61.7 7.4 %copy-start.1 = (f32[512,3,1536]{2,0,1:T(8,128)}, f32[512,3,1536]{2,0,1:T(8,128)S(1)}, u32[]{:S(2)}) copy-start(f32[512,3,1536]{2,0,1:T(8,128)S(1)} %get-tuple-element.107) | copy-start | bytes 28311556
  70.4 8.1 %copy-start.16 = (bf16[1,2048,128]{1,2,0:T(8,128)(2,1)S(1)}, bf16[1,2048,128]{1,2,0:T(8,128)(2,1)}, u32[]{:S(2)}) copy-start(bf16[1,2048,128]{1,2,0:T(8,128)(2,1)} %get-tuple-element.102) | copy-start | bytes 1572868
  70.4 11.3 %slice-start = ((s8[9437184]{0:T(1024)(128)(4,1)}), s8[1048576]{0:T(1024)(128)(4,1)S(1)}, s32[]{:S(2)}) async-start(s8[9437184]{0:T(1024)(128)(4,1)} %bitcast.278), calls=%async_computation.8 | async-start | bytes 2097152
  94.1 7.4 %copy-start.8 = (f32[512,3,512]{0,2,1:T(8,128)S(1)}, f32[512,3,512]{0,2,1:T(8,128)}, u32[]{:S(2)}) copy-start(f32[512,3,512]{0,2,1:T(8,128)} %copy-done.7) | copy-start | bytes 9437188
  94.2 7.4 %copy-start.17 = (bf16[1,2048,128]{1,2,0:T(8,128)(2,1)S(1)}, bf16[1,2048,128]{1,2,0:T(8,128)(2,1)}, u32[]{:S(2)}) copy-start(bf16[1,2048,128]{1,2,0:T(8,128)(2,1)} %get-tuple-element.102) | copy-start | bytes 1572868
  94.2 7.4 %copy-start.43 = (f32[512,3]{0,1:T(4,128)S(1)}, f32[512,3]{0,1:T(4,128)}, u32[]{:S(2)}) copy-start(f32[512,3]{0,1:T(4,128)} %copy-done.42) | copy-start | bytes 18436
  94.2 7.4 %copy-start.45 = (f32[512,3]{0,1:T(4,128)S(1)}, f32[512,3]{0,1:T(4,128)}, u32[]{:S(2)}) copy-start(f32[512,3]{0,1:T(4,128)} %copy-done.44) | copy-start | bytes 18436
  94.2 7.4 %copy-start.62 = (f32[512,3,64]{0,2,1:T(8,128)S(1)}, f32[512,3,64]{0,2,1:T(8,128)}, u32[]{:S(2)}) copy-start(f32[512,3,64]{0,2,1:T(8,128)} %get-tuple-element.118) | copy-start | bytes 1179652
  94.2 7.4 %copy-start.63 = (f32[512,3,64]{0,2,1:T(8,128)S(1)}, f32[512,3,64]{0,2,1:T(8,128)}, u32[]{:S(2)}) copy-start(f32[512,3,64]{0,2,1:T(8,128)} %get-tuple-element.116) | copy-start | bytes 1179652
  94.2 7.4 %copy-start.64 = (f32[512,3,64]{0,2,1:T(8,128)S(1)}, f32[512,3,64]{0,2,1:T(8,128)}, u32[]{:S(2)}) copy-start(f32[512,3,64]{0,2,1:T(8,128)} %get-tuple-element.114) | copy-start | bytes 1179652
  94.2 9.4 %slice-start.9 = ((s8[12582912]{0:T(1024)(128)(4,1)}), s8[4194304]{0:T(1024)(128)(4,1)S(1)}, s32[]{:S(2)}) async-start(s8[12582912]{0:T(1024)(128)(4,1)} %bitcast.284), calls=%async_computation.17 | async-start | bytes 8388608
  94.2 9.4 %slice-start.10 = ((s8[12582912]{0:T(1024)(128)(4,1)}), s8[4194304]{0:T(1024)(128)(4,1)S(1)}, s32[]{:S(2)}) async-start(s8[12582912]{0:T(1024)(128)(4,1)} %bitcast.284), calls=%async_computation.18 | async-start | bytes 8388608
  130.1 17.6 %copy-start.56 = (bf16[1,2048,768]{2,1,0:T(8,128)(2,1)S(1)}, bf16[1,2048,768]{2,1,0:T(8,128)(2,1)}, u32[]{:S(2)}) copy-start(bf16[1,2048,768]{2,1,0:T(8,128)(2,1)} %all-gather.5.cloned.1.call-done) | copy-start | bytes 9437188
  130.1 17.6 %copy-start.58 = (bf16[768,768]{1,0:T(8,128)(2,1)S(1)}, bf16[768,768]{1,0:T(8,128)(2,1)}, u32[]{:S(2)}) copy-start(bf16[768,768]{1,0:T(8,128)(2,1)} %param.31) | copy-start | bytes 3538948
  165.5 257.0 %all-reduce.7.cloned.1.call-start = ((), (), s32[]{:S(2)}) async-start(), calls=%async_computation.7 | async-start | bytes 5898240 | tf_op jit(solution)/shard_map/psum | solution.py:236
  179.7 282.0 %reduce-scatter.5.cloned.1.call-start = ((), (), s32[]{:S(2)}) async-start(), calls=%async_computation.5 | async-start | bytes 3932160 | tf_op jit(solution)/shard_map/reduce_scatter | solution.py:226
  180.3 321.9 %reduce-scatter.3.cloned.1.call-start = ((), (), s32[]{:S(2)}) async-start(), calls=%async_computation.3 | async-start | bytes 3932160 | tf_op jit(solution)/shard_map/reduce_scatter | solution.py:142
  188.3 314.0 %copy-start.11 = (bf16[1,512,768]{2,1,0:T(8,128)(2,1)S(1)}, bf16[1,512,768]{2,1,0:T(8,128)(2,1)}, u32[]{:S(2)}) copy-start(bf16[1,512,768]{2,1,0:T(8,128)(2,1)} %param.24) | copy-start | bytes 2359300
  (53 other events, 179.6 us)
Sparse Core Ops, SparseCore 0:
  9.6 31.2 all-gather.2
  43.0 28.6 all-gather.4
  165.6 125.9 all-reduce.4
  296.6 125.8 all-reduce.6
  424.8 36.7 reduce-scatter.4
  464.2 37.9 reduce-scatter.2
where the time goes:
time: 517 us; the launch traced here: 513 us
  waiting for transfers between devices  324 us (63%)
  matrix products  111 us (21%)
  other arithmetic  49.1 us (9%)
  between operations  16.2 us (3%)
  local copies, waits for them, and re-layouts  11.6 us (2%)
    psum x1, waiting for transfers between devices, shards(): lax.psum(tuple((v.astype(jnp.bfloat16) for v in (grad_query, grad_output,...  128 us
    psum x1, waiting for transfers between devices, shards(): lax.psum(jnp.concatenate([grad_keyval.reshape(-1), small.reshape(-1)]).re...  103 us
    reduce_scatter x1, waiting for transfers between devices, shards(): lax.psum_scatter((attention_branch + feedforward_branch).astype(jnp.bfloa...  38.7 us
    reduce_scatter x1, waiting for transfers between devices, shards(): lax.psum_scatter((part_one * norm_gain_one + norm_part_two * norm_gain_tw...  29.9 us
    all_gather x1, waiting for transfers between devices, shards(): lax.all_gather(tokens, 'tp', axis=1, tiled=True).astype(jnp.float32)  23.9 us
    dot_general x1, matrix products, shards(): jnp.dot(rows_two, up_weight, preferred_element_type=jnp.float32)  17.6 us
    dot_general x5, matrix products, against(): lax.dot_general(left, weight, (((2,), (1,)), ((), ())), preferred_element...  15 us
    dot_general x5, matrix products, outer_sum(): lax.dot_general(left, right, (((0, 1), (0, 1)), ((), ())), preferred_elem...  14.9 us
  transfers between devices with their start and end apart: 6, of which 5 were waited for; matrix products, arithmetic and copies ran while one was open for 17% of the time, Pallas kernels for 0%

commit v1 on v0

--- a/solution.py
+++ b/solution.py
@@ -243,8 +243,12 @@
             "dp",
         )
     ]
-    tail = lax.psum(
-        jnp.concatenate([grad_keyval.reshape(-1), small.reshape(-1)]).reshape(-1, 128), ("dp", "tp")
+    tail = jnp.sum(
+        lax.all_gather(
+            jnp.concatenate([grad_keyval.reshape(-1), small.reshape(-1)]).reshape(-1, 128),
+            ("dp", "tp"),
+        ),
+        axis=0,
     ).reshape(-1)
     grad_keyval, small = (
         tail[: grad_keyval.size].reshape(grad_keyval.shape),

time: 517 us -> 487 us (0.942)
  waiting for transfers between devices: 324 us -> 292 us
  other arithmetic: 49.1 us -> 54.4 us
    psum x1 -> x0, waiting for transfers between devices: 103 us -> none  [shards(): lax.psum(jnp.concatenate([grad_keyval.reshape(-1), small.reshape(-1)]).re...]
    all_gather x0 -> x1, waiting for transfers between devices: none -> 97.3 us  [shards(): lax.all_gather(jnp.concatenate([grad_keyval.reshape(-1), small.reshape(-1...]
    psum x1, waiting for transfers between devices: 128 us -> 102 us  [shards(): lax.psum(tuple((v.astype(jnp.bfloat16) for v in (grad_query, grad_output,...]
    reduce_sum x0 -> x1, other arithmetic: none -> 5.3 us  [shards(): jnp.sum(lax.all_gather(jnp.concatenate([grad_keyval.reshape(-1), small.re...]
  transfers between devices with their start and end apart: 6 -> 6, of which waited for: 5 -> 5; matrix products, arithmetic and copies ran while one was open for 17% -> 19% of each run, Pallas kernels for 0% -> 0%
where the time goes in v1:
time: 487 us; the launch traced here: 483 us
  waiting for transfers between devices  292 us (60%)
  matrix products  111 us (23%)
  other arithmetic  54.4 us (11%)
  between operations  16.3 us (3%)
  local copies, waits for them, and re-layouts  8.89 us (2%)
    psum x1, waiting for transfers between devices, shards(): lax.psum(tuple((v.astype(jnp.bfloat16) for v in (grad_query, grad_output,...  102 us
    all_gather x1, waiting for transfers between devices, shards(): lax.all_gather(jnp.concatenate([grad_keyval.reshape(-1), small.reshape(-1...  97.3 us
    reduce_scatter x1, waiting for transfers between devices, shards(): lax.psum_scatter((attention_branch + feedforward_branch).astype(jnp.bfloa...  38.5 us
    reduce_scatter x1, waiting for transfers between devices, shards(): lax.psum_scatter((part_one * norm_gain_one + norm_part_two * norm_gain_tw...  30 us
    all_gather x1, waiting for transfers between devices, shards(): lax.all_gather(tokens, 'tp', axis=1, tiled=True).astype(jnp.float32)  23.9 us
    dot_general x1, matrix products, shards(): jnp.dot(rows_two, up_weight, preferred_element_type=jnp.float32)  16.3 us
    dot_general x5, matrix products, against(): lax.dot_general(left, weight, (((2,), (1,)), ((), ())), preferred_element...  16.2 us
    dot_general x5, matrix products, outer_sum(): lax.dot_general(left, right, (((0, 1), (0, 1)), ((), ())), preferred_elem...  14.1 us
  transfers between devices with their start and end apart: 6, of which 5 were waited for; matrix products, arithmetic and copies ran while one was open for 19% of the time, Pallas kernels for 0%

profile of v1, /device:TPU:0, one launch (start us, length us, event | category | flops | bytes accessed | tf_op | source)
XLA Modules:
  0.0 483.0 jit_solution(11907704233770937463)
XLA Ops:
  9.9 2.8 fusion.102
  17.0 23.9 %all-gather.4.cloned.1.call-done = bf16[1,2048,768]{2,1,0:T(8,128)(2,1)} async-done(((bf16[1,512,768]{2,1,0:T(8,128)(2,1)}), bf16[1,2048,768]{2,1,0:T(8,128)(2,1)}) %all-gather.4.cloned.1.call-update) | async-done | bytes 3145744 | tf_op jit(solution)/shard_map/all_gather | solution.py:86
  40.9 2.5 convert_reduce_fusion
  43.4 2.9 fusion.17
  61.8 6.3 %fusion.10 = (f32[512,3]{0,1:T(4,128)S(1)}, f32[512,3,2048]{2,0,1:T(8,128)}) fusion(pred[512,2048]{1,0:T(8,128)(4,1)S(1)} %iota_compare_fusion, bf16[1,2048,1,48]{1,3,2,0:T(8,128)(2,1)S(1)} %slice.387, bf16[1,2048,1,8]{1,3,2,0:T(8,128)(2,1)S(1)} %get-tuple-element.92, bf16[1,2048,1,8]{1,3,2,0:T(8,128)(2,1)S(1)} %get-tuple-element.91, ...), kind=kOutput, calls=%fused_computation.25 | convolution fusion | flops 412875264 | bytes 14096384 | tf_op jit(solution)/shard_map/sqhd,skd->sqhk/dot_general | solution.py:106
  70.6 6.9 %fusion = f32[512,3]{0,1:T(4,128)S(1)} fusion(f32[512,3,2048]{2,0,1:T(8,128)} %get-tuple-element.109, f32[512,3]{0,1:T(4,128)S(1)} %get-tuple-element.108, pred[512,2048]{1,0:T(8,128)(4,1)S(1)} %iota_compare_fusion), kind=kLoop, calls=%fused_computation.6 | loop fusion | flops 12581376 | bytes 13643776 | tf_op jit(solution)/shard_map/reduce_sum | solution.py:125
  78.7 3.4 fusion.194
  82.3 2.9 fusion.193
  86.4 4.8 fusion.192
  91.2 3.1 fusion.71
  94.4 7.3 %fusion.80 = f32[1,2048,64]{1,2,0:T(8,128)} fusion(f32[512,3,2048]{2,0,1:T(8,128)} %get-tuple-element.109, f32[512,3]{0,1:T(4,128)S(1)} %copy-done.54, pred[512,2048]{1,0:T(8,128)(4,1)S(1)} %iota_compare_fusion, bf16[1,2048,3,64]{1,3,2,0:T(8,128)(2,1)S(1)} %bitcast.290), kind=kOutput, calls=%fused_computation.113 | convolution fusion | flops 415236096 | bytes 14360576 | tf_op jit(solution)/shard_map/sqhk,sqhd->skd/dot_general | solution.py:196
  104.5 4.4 multiply_convert_fusion
  117.2 2.4 multiply_convert_fusion.2
  123.1 2.5 multiply_convert_fusion.1
  131.9 16.3 %fusion.20 = (bf16[2048,768]{1,0:T(8,128)(2,1)S(1)}, f32[2048,768]{1,0:T(8,128)S(1)}) fusion(bf16[768,768]{1,0:T(8,128)(2,1)S(1)} %copy-done, bf16[1,2048,768]{2,1,0:T(8,128)(2,1)S(1)} %copy-done.3, f32[768]{0:T(1024)S(1)} %copy-done.63, f32[768]{0:T(1024)S(1)} %copy-done.59, f32[2048]{0:T(1024)S(1)} %copy-done.43, f32[2048]{0:T(1024)S(1)} %broadcast_multiply_fusion.1), kind=kOutput, calls=%fused_computation.35 | convolution fusion | flops 2527592448 | bytes 13785088 | tf_op jit(solution)/shard_map/dot_general | solution.py:139
  148.2 5.4 %fusion.26 = bf16[2048,768]{1,0:T(8,128)(2,1)S(1)} fusion(f32[2048,768]{1,0:T(8,128)S(1)} %get-tuple-element.112, bf16[768,768]{1,0:T(8,128)(2,1)S(1)} %copy-done.62, bf16[1,2048,768]{2,1,0:T(8,128)(2,1)S(1)} %copy-done.61), kind=kOutput, calls=%fused_computation.41 | convolution fusion | flops 2431647744 | bytes 13762560 | tf_op jit(solution)/shard_map/dot_general | solution.py:53
  153.6 4.3 convolution_convert_fusion
  157.9 3.7 fusion.104
  165.5 2.7 fusion.197
  168.2 2.9 fusion.15
  171.2 2.8 fusion.188
  174.3 4.9 %fusion.195 = f32[2048,768]{1,0:T(8,128)S(1)} fusion(bf16[2048,768]{1,0:T(8,128)(2,1)} %copy-done.64, bf16[768,768]{1,0:T(8,128)(2,1)} %param.31), kind=kOutput, calls=%fused_computation.293 | convolution fusion | flops 2415919104 | bytes 10616832 | tf_op jit(solution)/shard_map/dot_general | solution.py:141
  179.3 2.7 fusion.65
  182.1 3.0 convolution_bitcast_fusion
  186.5 101.8 %all-reduce.4.cloned.1.call-done = (bf16[768,192]{0,1:T(8,128)(2,1)}, bf16[192,768]{1,0:T(8,128)(2,1)}, bf16[768,768]{1,0:T(8,128)(2,1)}, bf16[768,768]{1,0:T(8,128)(2,1)}) async-done(((bf16[768,192]{0,1:T(8,128)(2,1)}, bf16[192,768]{1,0:T(8,128)(2,1)}, bf16[768,768]{1,0:T(8,128)(2,1)}, bf16[768,768]{1,0:T(8,128)(2,1)}), (bf16[768,192]{0,1:T(8,128)(2,1)}, bf16[192,768]{1,0:T(8,128)(2,1)}, ...) | async-done | bytes 2949136 | tf_op jit(solution)/shard_map/psum | solution.py:236
  292.0 2.8 convert_element_type.267
  294.8 2.9 convert_element_type.269
  297.7 30.0 %reduce-scatter.5.cloned.1.call-done = bf16[1,512,768]{2,1,0:T(8,128)(2,1)} async-done(((bf16[1,2048,768]{2,1,0:T(8,128)(2,1)}), bf16[1,512,768]{2,1,0:T(8,128)(2,1)}) %reduce-scatter.5.cloned.1.call-update) | async-done | bytes 786448 | tf_op jit(solution)/shard_map/reduce_scatter | solution.py:226
  329.6 38.5 %reduce-scatter.3.cloned.1.call-done = bf16[1,512,768]{2,1,0:T(8,128)(2,1)} async-done(((bf16[1,2048,768]{2,1,0:T(8,128)(2,1)}), bf16[1,512,768]{2,1,0:T(8,128)(2,1)}) %reduce-scatter.3.cloned.1.call-update) | async-done | bytes 786448 | tf_op jit(solution)/shard_map/reduce_scatter | solution.py:142
  368.1 3.8 fusion.93
  371.9 97.3 %all-gather.8.cloned.1.call-done = f32[32,792,128]{2,1,0:T(8,128)} async-done(((f32[1,792,128]{2,1,0:T(8,128)}), f32[32,792,128]{2,1,0:T(8,128)}) %all-gather.8.cloned.1.call-update) | async-done | bytes 12976144 | tf_op jit(solution)/shard_map/all_gather | solution.py:247
  469.3 5.3 %reduce_sum.199 = f32[792,128]{1,0:T(8,128)S(1)} reduce(f32[32,792,128]{2,1,0:T(8,128)} %all-gather.8.cloned.1.call-done, f32[]{:T(128)} %constant.169.clone.1), dimensions={0}, to_apply=%region_26.27 | reduce | flops 3142656 | bytes 13381636 | tf_op jit(solution)/shard_map/reduce_sum | solution.py:246
  (264 shorter events, 59.4 us)
Async XLA Ops:
  7.2 124.6 %copy-start = (bf16[768,768]{1,0:T(8,128)(2,1)S(1)}, bf16[768,768]{1,0:T(8,128)(2,1)}, u32[]{:S(2)}) copy-start(bf16[768,768]{1,0:T(8,128)(2,1)} %param.30) | copy-start | bytes 3538948
  7.2 39.8 %copy-start.50 = (f32[768]{0:T(1024)S(1)}, f32[768]{0:T(1024)}, u32[]{:S(2)}) copy-start(f32[768]{0:T(1024)} %param.32) | copy-start | bytes 9220
  7.2 39.8 %copy-start.58 = (f32[768]{0:T(1024)S(1)}, f32[768]{0:T(1024)}, u32[]{:S(2)}) copy-start(f32[768]{0:T(1024)} %param.33) | copy-start | bytes 9220
  7.2 33.7 %all-gather.4.cloned.1.call-start = ((), (), s32[]{:S(2)}) async-start(), calls=%async_computation.2 | async-start | bytes 3932160 | tf_op jit(solution)/shard_map/all_gather | solution.py:86
  7.9 83.2 %all-gather.6.cloned.1.call-start = ((), (), s32[]{:S(2)}) async-start(), calls=%async_computation.4 | async-start | bytes 3932160 | tf_op jit(solution)/shard_map/all_gather | solution.py:87
  12.7 275.6 %all-reduce.4.cloned.1.call-start = ((), (), s32[]{:S(2)}) async-start(), calls=%async_computation.7 | async-start | bytes 5898240 | tf_op jit(solution)/shard_map/psum | solution.py:236
  12.8 28.1 %copy-start.55 = (f32[8]{0:T(128)}, f32[8]{0:T(128)S(1)}, u32[]{:S(2)}) copy-start(f32[8]{0:T(128)S(1)} %multiply_power_fusion) | copy-start | bytes 100
  17.0 35.3 %copy-start.18 = (f32[2048,8]{0,1:T(8,128)}, f32[2048,8]{0,1:T(8,128)S(1)}, u32[]{:S(2)}) copy-start(f32[2048,8]{0,1:T(8,128)S(1)} %get-tuple-element.99) | copy-start | bytes 196612
  17.0 31.6 %copy-start.20 = (bf16[768,128]{1,0:T(8,128)(2,1)S(1)}, bf16[768,128]{1,0:T(8,128)(2,1)}, u32[]{:S(2)}) copy-start(bf16[768,128]{1,0:T(8,128)(2,1)} %param.28) | copy-start | bytes 589828
  51.0 10.8 %copy-start.25 = (bf16[1,2048,1,8]{1,3,2,0:T(8,128)(2,1)}, bf16[1,2048,1,8]{1,3,2,0:T(8,128)(2,1)S(1)}, u32[]{:S(2)}) copy-start(bf16[1,2048,1,8]{1,3,2,0:T(8,128)(2,1)S(1)} %get-tuple-element.91) | copy-start | bytes 98308
  51.0 10.8 %copy-start.27 = (bf16[1,2048,1,8]{1,3,2,0:T(8,128)(2,1)}, bf16[1,2048,1,8]{1,3,2,0:T(8,128)(2,1)S(1)}, u32[]{:S(2)}) copy-start(bf16[1,2048,1,8]{1,3,2,0:T(8,128)(2,1)S(1)} %get-tuple-element.92) | copy-start | bytes 98308
  51.0 10.7 %copy-start.12 = (bf16[1,2048,1,48]{1,3,2,0:T(8,128)(2,1)}, bf16[1,2048,1,48]{1,3,2,0:T(8,128)(2,1)S(1)}, u32[]{:S(2)}) copy-start(bf16[1,2048,1,48]{1,3,2,0:T(8,128)(2,1)S(1)} %slice.387) | copy-start | bytes 589828
  57.2 21.4 %copy-start.10 = (f32[512,3,1024]{2,0,1:T(8,128)}, f32[512,3,1024]{2,0,1:T(8,128)S(1)}, u32[]{:S(2)}) copy-start(f32[512,3,1024]{2,0,1:T(8,128)S(1)} %get-tuple-element.105) | copy-start | bytes 18874372
  61.8 7.4 %copy-start.1 = (f32[512,3,1536]{2,0,1:T(8,128)}, f32[512,3,1536]{2,0,1:T(8,128)S(1)}, u32[]{:S(2)}) copy-start(f32[512,3,1536]{2,0,1:T(8,128)S(1)} %get-tuple-element.107) | copy-start | bytes 28311556
  70.6 8.1 %copy-start.16 = (bf16[1,2048,128]{1,2,0:T(8,128)(2,1)S(1)}, bf16[1,2048,128]{1,2,0:T(8,128)(2,1)}, u32[]{:S(2)}) copy-start(bf16[1,2048,128]{1,2,0:T(8,128)(2,1)} %get-tuple-element.102) | copy-start | bytes 1572868
  70.6 11.6 %slice-start = ((s8[9437184]{0:T(1024)(128)(4,1)}), s8[1048576]{0:T(1024)(128)(4,1)S(1)}, s32[]{:S(2)}) async-start(s8[9437184]{0:T(1024)(128)(4,1)} %bitcast.278), calls=%async_computation.8 | async-start | bytes 2097152
  94.3 7.4 %copy-start.8 = (f32[512,3,512]{0,2,1:T(8,128)S(1)}, f32[512,3,512]{0,2,1:T(8,128)}, u32[]{:S(2)}) copy-start(f32[512,3,512]{0,2,1:T(8,128)} %copy-done.7) | copy-start | bytes 9437188
  94.3 7.4 %copy-start.17 = (bf16[1,2048,128]{1,2,0:T(8,128)(2,1)S(1)}, bf16[1,2048,128]{1,2,0:T(8,128)(2,1)}, u32[]{:S(2)}) copy-start(bf16[1,2048,128]{1,2,0:T(8,128)(2,1)} %get-tuple-element.102) | copy-start | bytes 1572868
  94.3 7.4 %copy-start.47 = (f32[512,3]{0,1:T(4,128)S(1)}, f32[512,3]{0,1:T(4,128)}, u32[]{:S(2)}) copy-start(f32[512,3]{0,1:T(4,128)} %copy-done.46) | copy-start | bytes 18436
  94.3 7.4 %copy-start.49 = (f32[512,3]{0,1:T(4,128)S(1)}, f32[512,3]{0,1:T(4,128)}, u32[]{:S(2)}) copy-start(f32[512,3]{0,1:T(4,128)} %copy-done.48) | copy-start | bytes 18436
  94.3 7.4 %copy-start.67 = (f32[512,3,64]{0,2,1:T(8,128)S(1)}, f32[512,3,64]{0,2,1:T(8,128)}, u32[]{:S(2)}) copy-start(f32[512,3,64]{0,2,1:T(8,128)} %get-tuple-element.118) | copy-start | bytes 1179652
  94.3 7.4 %copy-start.68 = (f32[512,3,64]{0,2,1:T(8,128)S(1)}, f32[512,3,64]{0,2,1:T(8,128)}, u32[]{:S(2)}) copy-start(f32[512,3,64]{0,2,1:T(8,128)} %get-tuple-element.116) | copy-start | bytes 1179652
  94.3 7.4 %copy-start.69 = (f32[512,3,64]{0,2,1:T(8,128)S(1)}, f32[512,3,64]{0,2,1:T(8,128)}, u32[]{:S(2)}) copy-start(f32[512,3,64]{0,2,1:T(8,128)} %get-tuple-element.114) | copy-start | bytes 1179652
  94.4 9.4 %slice-start.9 = ((s8[12582912]{0:T(1024)(128)(4,1)}), s8[4194304]{0:T(1024)(128)(4,1)S(1)}, s32[]{:S(2)}) async-start(s8[12582912]{0:T(1024)(128)(4,1)} %bitcast.284), calls=%async_computation.17 | async-start | bytes 8388608
  94.4 9.4 %slice-start.10 = ((s8[12582912]{0:T(1024)(128)(4,1)}), s8[4194304]{0:T(1024)(128)(4,1)S(1)}, s32[]{:S(2)}) async-start(s8[12582912]{0:T(1024)(128)(4,1)} %bitcast.284), calls=%async_computation.18 | async-start | bytes 8388608
  131.8 16.3 %copy-start.61 = (bf16[1,2048,768]{2,1,0:T(8,128)(2,1)S(1)}, bf16[1,2048,768]{2,1,0:T(8,128)(2,1)}, u32[]{:S(2)}) copy-start(bf16[1,2048,768]{2,1,0:T(8,128)(2,1)} %all-gather.6.cloned.1.call-done) | copy-start | bytes 9437188
  131.8 16.3 %copy-start.62 = (bf16[768,768]{1,0:T(8,128)(2,1)S(1)}, bf16[768,768]{1,0:T(8,128)(2,1)}, u32[]{:S(2)}) copy-start(bf16[768,768]{1,0:T(8,128)(2,1)} %param.31) | copy-start | bytes 3538948
  148.1 9.7 %copy-start.64 = (bf16[2048,768]{1,0:T(8,128)(2,1)}, bf16[2048,768]{1,0:T(8,128)(2,1)S(1)}, u32[]{:S(2)}) copy-start(bf16[2048,768]{1,0:T(8,128)(2,1)S(1)} %get-tuple-element.111) | copy-start | bytes 9437188
  163.2 164.6 %reduce-scatter.5.cloned.1.call-start = ((), (), s32[]{:S(2)}) async-start(), calls=%async_computation.5 | async-start | bytes 3932160 | tf_op jit(solution)/shard_map/reduce_scatter | solution.py:226
  174.0 194.0 %reduce-scatter.3.cloned.1.call-start = ((), (), s32[]{:S(2)}) async-start(), calls=%async_computation.3 | async-start | bytes 3932160 | tf_op jit(solution)/shard_map/reduce_scatter | solution.py:142
  182.0 287.3 %all-gather.8.cloned.1.call-start = ((), (), s32[]{:S(2)}) async-start(), calls=%async_computation.6 | async-start | bytes 13381632 | tf_op jit(solution)/shard_map/all_gather | solution.py:247
  185.9 182.2 %copy-start.11 = (bf16[1,512,768]{2,1,0:T(8,128)(2,1)S(1)}, bf16[1,512,768]{2,1,0:T(8,128)(2,1)}, u32[]{:S(2)}) copy-start(bf16[1,512,768]{2,1,0:T(8,128)(2,1)} %param.24) | copy-start | bytes 2359300
  (58 other events, 199.8 us)
Sparse Core Ops, SparseCore 0:
  9.6 31.2 all-gather.3
  43.0 28.5 all-gather.5
  163.3 124.9 all-reduce.3
  290.9 36.7 reduce-scatter.4
  330.1 37.9 reduce-scatter.2
  371.3 97.9 all-gather.7
